TPU v7x, 128 devices: a whole 4x4x4 slice. The times are simulated.
128 devices in a mesh: shot: 4 (over z), row: 8 (over x, y_lo), col: 4 (over y_hi, core).
Axes of the slice: x: 4, y: 4 (y_hi: 2, y_lo: 2; y = y_hi * 2 + y_lo), z: 4, core: 2. Of those that a mesh axis runs over, the one named last changes fastest.
Arguments:
- velocity: float32 [256, 256, 384], P(('row', 'shot'), 'col'), may hold values from 1.5 to 4.5
- momentum: float32 [256, 256, 384], P(('row', 'shot'), 'col'), may hold values from -6 to 6
- mass_diag: float32 [256, 256, 384], P(('row', 'shot'), 'col'), may hold values from 0.5 to 2
- u_prev: float32 [4, 256, 256, 384], P('shot', 'row', 'col'), may hold values from -6 to 6
- u_cur: float32 [4, 256, 256, 384], P('shot', 'row', 'col'), may hold values from -6 to 6
- adj_next: float32 [4, 256, 256, 384], P('shot', 'row', 'col'), may hold values from -6 to 6
- adj_cur: float32 [4, 256, 256, 384], P('shot', 'row', 'col'), may hold values from -6 to 6
- observed: float32 [4, 2, 256, 256], P('shot', None, 'row', 'col'), may hold values from -6 to 6
- rec_depth: int32 [4, 256, 256], P('shot', 'row', 'col'), may hold values from 0 to 383
- src_cell: int32 [4, 3], P('shot'), may hold values from 0 to 255
- wavelet: float32 [4, 2], P('shot'), may hold values from -60 to 60
Outputs:
- v_new: float32 [256, 256, 384], P(('row', 'shot'), 'col')
- p_half: float32 [256, 256, 384], P(('row', 'shot'), 'col')
All inputs are finite; a program needn't handle non-finite values.
Results may differ from a plain program's by a relative error of at most 0.0001.
Values sent between devices are 32-bit elements; how exact they have to be, the bound alone decides.
A program may use at most 128 MiB of HBM per device.

v0:
```python
import jax
import jax.numpy as jnp
from jax import lax
from jax.sharding import PartitionSpec as P

STENCIL = (-205.0 / 72.0, 8.0 / 5.0, -1.0 / 5.0, 8.0 / 315.0, -1.0 / 560.0)
squared_courant = 0.012
leap_step = 0.2


def extended(block, sides, width):
    for axis, dim in sides:
        count = lax.axis_size(axis)
        forward = [(i, i + 1) for i in range(count - 1)]
        backward = [(target, source) for source, target in forward]
        low = lax.ppermute(
            lax.slice_in_dim(block, block.shape[dim] - width, None, axis=dim), axis, forward
        )
        high = lax.ppermute(lax.slice_in_dim(block, 0, width, axis=dim), axis, backward)
        block = jnp.concatenate([low, block, high], axis=dim)
    return block


def laplace(padded):
    row_count = padded.shape[0] - 8
    col_count = padded.shape[1] - 8
    depth_cells = padded.shape[2]
    center = padded[4 : 4 + row_count, 4 : 4 + col_count]
    z_padded = jnp.pad(center, ((0, 0), (0, 0), (4, 4)))
    result = 3.0 * STENCIL[0] * center
    for offset in range(1, 5):
        along = (
            padded[4 + offset : 4 + offset + row_count, 4 : 4 + col_count]
            + padded[4 - offset : 4 - offset + row_count, 4 : 4 + col_count]
        )
        along = (
            along
            + padded[4 : 4 + row_count, 4 + offset : 4 + offset + col_count]
            + padded[4 : 4 + row_count, 4 - offset : 4 - offset + col_count]
        )
        along = (
            along
            + z_padded[:, :, 4 + offset : 4 + offset + depth_cells]
            + z_padded[:, :, 4 - offset : 4 - offset + depth_cells]
        )
        result = result + STENCIL[offset] * along
    return result


def with_faces(field):
    return extended(field, (("row", 0), ("col", 1)), 4)


def on_device(
    velocity,
    momentum,
    mass_diag,
    u_prev,
    u_cur,
    adj_next,
    adj_cur,
    observed,
    rec_depth,
    src_cell,
    wavelet,
):
    full_velocity = lax.all_gather(velocity, "shot", axis=0, tiled=True)
    stiffness = squared_courant * full_velocity * full_velocity
    row_count, col_count, depth_cells = full_velocity.shape
    oldest = u_prev[0]
    present = u_cur[0]
    adj_later = adj_next[0]
    adj_now = adj_cur[0]
    padded_wave = extended(present, (("row", 0), ("col", 1)), 4)
    padded_adjoint = extended(adj_now, (("row", 0), ("col", 1)), 4)
    x_index = lax.iota(jnp.int32, row_count) + lax.axis_index("row") * row_count
    y_index = lax.iota(jnp.int32, col_count) + lax.axis_index("col") * col_count
    z_index = lax.iota(jnp.int32, depth_cells)
    cell = src_cell[0]
    source_mask = (
        (x_index == cell[0])[:, None, None]
        & (y_index == cell[1])[None, :, None]
        & (z_index == cell[2])[None, None, :]
    ).astype(jnp.float32)
    advanced = (
        2.0 * present - oldest + stiffness * laplace(padded_wave) + wavelet[0, 0] * source_mask
    )
    farthest = (
        2.0 * advanced
        - present
        + stiffness * laplace(with_faces(advanced))
        + wavelet[0, 1] * source_mask
    )
    receiver_mask = (z_index[None, None, :] == rec_depth[0][:, :, None]).astype(jnp.float32)
    misfit_late = jnp.sum(farthest * receiver_mask, axis=2) - observed[0, 1]
    misfit_early = jnp.sum(advanced * receiver_mask, axis=2) - observed[0, 0]
    adj_two = (
        2.0 * adj_now
        - adj_later
        + stiffness * laplace(padded_adjoint)
        + misfit_late[:, :, None] * receiver_mask
    )
    adj_one = (
        2.0 * adj_two
        - adj_now
        + stiffness * laplace(with_faces(adj_two))
        + misfit_early[:, :, None] * receiver_mask
    )
    imaging = adj_two * (farthest - 2.0 * advanced + present) + adj_one * (
        advanced - 2.0 * present + oldest
    )
    share_rows = velocity.shape[0]
    full_sum = lax.psum(imaging, "shot")
    summed = lax.dynamic_slice_in_dim(full_sum, lax.axis_index("shot") * share_rows, share_rows, 0)
    gradient = 2.0 / velocity * summed
    p_half = momentum - 0.5 * leap_step * gradient
    v_new = velocity + leap_step * p_half / mass_diag
    return (v_new, p_half)


def solution(mesh):
    return jax.shard_map(
        on_device,
        mesh=mesh,
        in_specs=(
            P(("row", "shot"), "col", None),
            P(("row", "shot"), "col", None),
            P(("row", "shot"), "col", None),
            P("shot", "row", "col", None),
            P("shot", "row", "col", None),
            P("shot", "row", "col", None),
            P("shot", "row", "col", None),
            P("shot", None, "row", "col"),
            P("shot", "row", "col"),
            P("shot", None),
            P("shot", None),
        ),
        out_specs=(P(("row", "shot"), "col", None), P(("row", "shot"), "col", None)),
        check_vma=False,
    )
```

profile of v0, /device:TPU:1, one launch (start us, length us, event | category | flops | bytes accessed | tf_op | source)
XLA Modules:
  0.0 376.6 jit_solution(13717517673409891883)
XLA Ops:
  8.0 2.2 slice_bitcast_fusion.3
  11.5 5.4 %collective-permute-start.1 = (f32[4,64,384]{2,1,0:T(8,128)}, f32[4,64,384]{2,1,0:T(8,128)}, u32[]{:S(2)}, u32[]{:S(2)}) collective-permute-start(f32[4,64,384]{2,1,0:T(8,128)} %get-tuple-element.30), channel_id=1, source_target_pairs={{0,4},{4,8},{8,12},{12,16},{16,20},{20,24},{24,28},{1,5},{5,9},{9,... | collective-permute-start | bytes 1179656 | tf_op jit(solution)/shard_map/ppermute | solution.py:16
  20.3 4.9 %collective-permute-start.5 = (f32[4,64,384]{2,1,0:T(8,128)}, f32[4,64,384]{2,1,0:T(8,128)}, u32[]{:S(2)}, u32[]{:S(2)}) collective-permute-start(f32[4,64,384]{2,1,0:T(8,128)} %get-tuple-element.28), channel_id=1, source_target_pairs={{0,4},{4,8},{8,12},{12,16},{16,20},{20,24},{24,28},{1,5},{5,9},{9,... | collective-permute-start | bytes 1179656 | tf_op jit(solution)/shard_map/ppermute | solution.py:16
  27.7 3.3 collective-permute-done.4
  31.0 18.5 %collective-permute-done.5 = f32[4,64,384]{2,1,0:T(8,128)} collective-permute-done((f32[4,64,384]{2,1,0:T(8,128)}, f32[4,64,384]{2,1,0:T(8,128)}, u32[]{:S(2)}, u32[]{:S(2)}) %collective-permute-start.5) | collective-permute-done | bytes 393248 | tf_op jit(solution)/shard_map/ppermute | solution.py:16
  50.5 2.4 collective-permute-start.6
  52.9 4.7 %collective-permute-start.7 = (f32[40,4,384]{2,1,0:T(4,128)S(1)}, f32[40,4,384]{2,1,0:T(4,128)S(1)}, u32[]{:S(2)}, u32[]{:S(2)}) collective-permute-start(f32[40,4,384]{2,1,0:T(4,128)S(1)} %get-tuple-element.18), channel_id=1, source_target_pairs={{0,1},{1,2},{2,3},{4,5},{5,6},{6,7},{8,9},{9,10},{10,11},{12,13},{... | collective-permute-start | bytes 737288 | tf_op jit(solution)/shard_map/ppermute | solution.py:16
  60.7 5.9 %pad_maximum_fusion.1 = (f32[40,68,384]{2,1,0:T(8,128)}, f32[40,68,384]{2,1,0:T(8,128)}) fusion(f32[40,4,384]{2,1,0:T(4,128)S(1)} %collective-permute-done.6, f32[4,64,384]{2,1,0:T(8,128)} %collective-permute-done.4, f32[32,64,384]{2,1,0:T(8,128)S(1)} %bitcast.36, f32[4,64,384]{2,1,0:T(8,128)} %collective-permute-done.5, ...), kind=kLoop, calls=%fused_computation.59 | loop fusion | flops 6266880 | bytes 12779520 | tf_op jit(solution)/shard_map/concatenate | solution.py:20
  66.6 23.5 %fusion.75 = f32[32,64,384]{2,1,0:T(8,128)} fusion(f32[32,64,384]{2,1,0:T(8,128)S(1)} %bitcast.37, f32[4,64,384]{2,1,0:T(8,128)} %collective-permute-done.5, f32[4,64,384]{2,1,0:T(8,128)} %collective-permute-done.4, f32[40,68,384]{2,1,0:T(8,128)} %get-tuple-element.16, f32[40,68,384]{2,1,0:T(8,128)} %get-tuple-element.15, f32[1,32,64,384]{3,2,1,0:T(8,128)} %param.14, ...), kind=kLoop, calls=%fused_computation.166 | loop fusion | flops 36175872 | bytes 38537604 | tf_op jit(solution)/shard_map/add | solution.py:86
  91.5 4.1 %collective-permute-start.9 = (f32[4,64,384]{2,1,0:T(8,128)S(1)}, f32[4,64,384]{2,1,0:T(8,128)S(1)}, u32[]{:S(2)}, u32[]{:S(2)}) collective-permute-start(f32[4,64,384]{2,1,0:T(8,128)S(1)} %get-tuple-element.25), channel_id=1, source_target_pairs={{0,4},{4,8},{8,12},{12,16},{16,20},{20,24},{24,28},{1,5},{5,9},{9,... | collective-permute-start | bytes 1179656 | tf_op jit(solution)/shard_map/ppermute | solution.py:16
  100.3 6.8 %collective-permute-start.3 = (f32[40,4,384]{2,1,0:T(4,128)S(1)}, f32[40,4,384]{2,1,0:T(4,128)S(1)}, u32[]{:S(2)}, u32[]{:S(2)}) collective-permute-start(f32[40,4,384]{2,1,0:T(4,128)S(1)} %get-tuple-element.22), channel_id=1, source_target_pairs={{0,1},{1,2},{2,3},{4,5},{5,6},{6,7},{8,9},{9,10},{10,11},{12,13},{... | collective-permute-start | bytes 737288 | tf_op jit(solution)/shard_map/ppermute | solution.py:16
  111.2 5.3 %collective-permute-start.11 = (f32[40,4,384]{2,1,0:T(4,128)S(1)}, f32[40,4,384]{2,1,0:T(4,128)S(1)}, u32[]{:S(2)}, u32[]{:S(2)}) collective-permute-start(f32[40,4,384]{2,1,0:T(4,128)S(1)} %get-tuple-element.14), channel_id=1, source_target_pairs={{0,1},{1,2},{2,3},{4,5},{5,6},{6,7},{8,9},{9,10},{10,11},{12,13},{... | collective-permute-start | bytes 737288 | tf_op jit(solution)/shard_map/ppermute | solution.py:16
  116.5 5.8 %pad_maximum_fusion = (f32[40,68,384]{2,1,0:T(8,128)}, f32[40,68,384]{2,1,0:T(8,128)}) fusion(f32[40,4,384]{2,1,0:T(4,128)S(1)} %collective-permute-done.2, f32[4,64,384]{2,1,0:T(8,128)S(1)} %collective-permute-done, f32[32,64,384]{2,1,0:T(8,128)S(1)} %bitcast.40, f32[4,64,384]{2,1,0:T(8,128)} %collective-permute-done.1, ...), kind=kLoop, calls=%fused_computation.57 | loop fusion | flops 6266880 | bytes 12779520 | tf_op jit(solution)/shard_map/concatenate | solution.py:20
  122.4 4.7 %pad_maximum_fusion.2 = (f32[40,68,384]{2,1,0:T(8,128)}, f32[40,68,384]{2,1,0:T(8,128)}) fusion(f32[40,4,384]{2,1,0:T(4,128)S(1)} %collective-permute-done.10, f32[4,64,384]{2,1,0:T(8,128)S(1)} %collective-permute-done.8, f32[32,64,384]{2,1,0:T(8,128)S(1)} %copy-done.1, f32[4,64,384]{2,1,0:T(8,128)S(1)} %collective-permute-done.9, ...), kind=kLoop, calls=%fused_computation.61 | loop fusion | flops 6266880 | bytes 12779520 | tf_op jit(solution)/shard_map/concatenate | solution.py:20
  127.0 45.6 %select_reduce_fusion = (f32[32,64]{1,0:T(8,128)}, f32[32,64]{1,0:T(8,128)}, f32[32,64,384]{2,1,0:T(8,128)}) fusion(f32[32,64,384]{2,1,0:T(8,128)} %fusion.75, s32[32,64]{1,0:T(8,128)S(1)} %bitcast.41, f32[]{:T(128)} %bitcast.13, pred[384]{0:T(512)(128)(4,1)} %copy-done.15, pred[32,64]{1,0:T(8,128)(4,1)} %copy-done.13, ...), kind=kLoop, calls=%fused_computation.252 | loop fusion | flops 40103936 | bytes 38562180 | tf_op jit(solution)/shard_map/reduce_sum | solution.py:96
  174.0 43.2 %fusion.106 = f32[32,64,384]{2,1,0:T(8,128)} fusion(f32[32,64,384]{2,1,0:T(8,128)} %bitcast.39, f32[4,64,384]{2,1,0:T(8,128)} %collective-permute-done.1, f32[4,64,384]{2,1,0:T(8,128)S(1)} %collective-permute-done, f32[40,68,384]{2,1,0:T(8,128)} %get-tuple-element.20, f32[40,68,384]{2,1,0:T(8,128)} %get-tuple-element.19, f32[1,32,64,384]{3,2,1,0:T(8,128)} %param.16, ...), kind=kLoop, calls=%fused_computation.197 | loop fusion | flops 36175872 | bytes 38551552 | tf_op jit(solution)/shard_map/add | solution.py:98
  219.8 4.5 %collective-permute-start.13 = (f32[4,64,384]{2,1,0:T(8,128)S(1)}, f32[4,64,384]{2,1,0:T(8,128)S(1)}, u32[]{:S(2)}, u32[]{:S(2)}) collective-permute-start(f32[4,64,384]{2,1,0:T(8,128)S(1)} %get-tuple-element.24), channel_id=1, source_target_pairs={{0,4},{4,8},{8,12},{12,16},{16,20},{20,24},{24,28},{1,5},{5,9},{9,... | collective-permute-start | bytes 1179656 | tf_op jit(solution)/shard_map/ppermute | solution.py:16
  224.3 4.9 %collective-permute-done.12 = f32[4,64,384]{2,1,0:T(8,128)S(1)} collective-permute-done((f32[4,64,384]{2,1,0:T(8,128)S(1)}, f32[4,64,384]{2,1,0:T(8,128)S(1)}, u32[]{:S(2)}, u32[]{:S(2)}) %collective-permute-start.12) | collective-permute-done | bytes 393248 | tf_op jit(solution)/shard_map/ppermute | solution.py:19
  229.2 9.2 %collective-permute-done.13 = f32[4,64,384]{2,1,0:T(8,128)S(1)} collective-permute-done((f32[4,64,384]{2,1,0:T(8,128)S(1)}, f32[4,64,384]{2,1,0:T(8,128)S(1)}, u32[]{:S(2)}, u32[]{:S(2)}) %collective-permute-start.13) | collective-permute-done | bytes 393248 | tf_op jit(solution)/shard_map/ppermute | solution.py:16
  241.9 5.4 %collective-permute-start.15 = (f32[40,4,384]{2,1,0:T(4,128)S(1)}, f32[40,4,384]{2,1,0:T(4,128)S(1)}, u32[]{:S(2)}, u32[]{:S(2)}) collective-permute-start(f32[40,4,384]{2,1,0:T(4,128)S(1)} %get-tuple-element.10), channel_id=1, source_target_pairs={{0,1},{1,2},{2,3},{4,5},{5,6},{6,7},{8,9},{9,10},{10,11},{12,13},{... | collective-permute-start | bytes 737288 | tf_op jit(solution)/shard_map/ppermute | solution.py:16
  250.3 3.7 pad_maximum_fusion.3
  254.0 32.6 %fusion.13 = f32[32,64,384]{2,1,0:T(8,128)} fusion(f32[32,64,384]{2,1,0:T(8,128)} %fusion.106, f32[4,64,384]{2,1,0:T(8,128)} %copy-done.7, f32[4,64,384]{2,1,0:T(8,128)S(1)} %collective-permute-done.12, f32[40,68,384]{2,1,0:T(8,128)} %get-tuple-element.8, f32[40,68,384]{2,1,0:T(8,128)S(1)} %get-tuple-element.7, f32[1,32,64,384]{3,2,1,0:T(8,128)} %param.14, ...), kind=kLoop, calls=%fused_computation.104 | loop fusion | flops 43253760 | bytes 51134464 | tf_op jit(solution)/shard_map/add | solution.py:109
  286.6 80.5 %all-reduce.6.cloned.1.call-done = f32[32,64,384]{2,1,0:T(8,128)} async-done(((f32[32,64,384]{2,1,0:T(8,128)}), f32[32,64,384]{2,1,0:T(8,128)}) %all-reduce.6.cloned.1.call-update) | async-done | bytes 3145744 | tf_op jit(solution)/shard_map/psum | solution.py:113
  367.2 2.6 divide_add_fusion
  (72 shorter events, 32.5 us)
Async XLA Ops:
  7.2 42.4 %copy-start = (f32[1,32,64,384]{3,2,1,0:T(8,128)S(1)}, f32[1,32,64,384]{3,2,1,0:T(8,128)}, u32[]{:S(2)}) copy-start(f32[1,32,64,384]{3,2,1,0:T(8,128)} %param.15) | copy-start | bytes 9437188
  7.2 59.4 %all-gather.2.cloned.1.call-start = ((), (), s32[]{:S(2)}) async-start(), calls=%async_computation | async-start | bytes 3932160 | tf_op jit(solution)/shard_map/all_gather | solution.py:67
  7.9 359.2 %all-reduce.6.cloned.1.call-start = ((), (), s32[]{:S(2)}) async-start(), calls=%async_computation.1 | async-start | bytes 6291456 | tf_op jit(solution)/shard_map/psum | solution.py:113
  10.2 86.7 %collective-permute-start = (f32[4,64,384]{2,1,0:T(8,128)}, f32[4,64,384]{2,1,0:T(8,128)S(1)}, u32[]{:S(2)}, u32[]{:S(2)}) collective-permute-start(f32[4,64,384]{2,1,0:T(8,128)} %get-tuple-element.29), channel_id=1, source_target_pairs={{4,0},{8,4},{12,8},{16,12},{20,16},{24,20},{28,24},{5,1},{9,5},{13... | collective-permute-start | bytes 1179656 | tf_op jit(solution)/shard_map/ppermute | solution.py:19
  11.5 85.4 %collective-permute-start.1 = (f32[4,64,384]{2,1,0:T(8,128)}, f32[4,64,384]{2,1,0:T(8,128)}, u32[]{:S(2)}, u32[]{:S(2)}) collective-permute-start(f32[4,64,384]{2,1,0:T(8,128)} %get-tuple-element.30), channel_id=1, source_target_pairs={{0,4},{4,8},{8,12},{12,16},{16,20},{20,24},{24,28},{1,5},{5,9},{9,... | collective-permute-start | bytes 1179656 | tf_op jit(solution)/shard_map/ppermute | solution.py:16
  19.0 12.0 %collective-permute-start.4 = (f32[4,64,384]{2,1,0:T(8,128)}, f32[4,64,384]{2,1,0:T(8,128)}, u32[]{:S(2)}, u32[]{:S(2)}) collective-permute-start(f32[4,64,384]{2,1,0:T(8,128)} %get-tuple-element.27), channel_id=1, source_target_pairs={{4,0},{8,4},{12,8},{16,12},{20,16},{24,20},{28,24},{5,1},{9,5},{13... | collective-permute-start | bytes 1179656 | tf_op jit(solution)/shard_map/ppermute | solution.py:19
  20.3 29.2 %collective-permute-start.5 = (f32[4,64,384]{2,1,0:T(8,128)}, f32[4,64,384]{2,1,0:T(8,128)}, u32[]{:S(2)}, u32[]{:S(2)}) collective-permute-start(f32[4,64,384]{2,1,0:T(8,128)} %get-tuple-element.28), channel_id=1, source_target_pairs={{0,4},{4,8},{8,12},{12,16},{16,20},{20,24},{24,28},{1,5},{5,9},{9,... | collective-permute-start | bytes 1179656 | tf_op jit(solution)/shard_map/ppermute | solution.py:16
  26.5 40.2 %copy-start.15 = (pred[384]{0:T(512)(128)(4,1)}, pred[384]{0:T(512)(128)(4,1)S(1)}, u32[]{:S(2)}) copy-start(pred[384]{0:T(512)(128)(4,1)S(1)} %iota_compare_fusion.1) | copy-start | bytes 1156
  50.5 9.0 %collective-permute-start.6 = (f32[40,4,384]{2,1,0:T(4,128)S(1)}, f32[40,4,384]{2,1,0:T(4,128)S(1)}, u32[]{:S(2)}, u32[]{:S(2)}) collective-permute-start(f32[40,4,384]{2,1,0:T(4,128)S(1)} %get-tuple-element.17), channel_id=1, source_target_pairs={{1,0},{2,1},{3,2},{5,4},{6,5},{7,6},{9,8},{10,9},{11,10},{13,12},{... | collective-permute-start | bytes 737288 | tf_op jit(solution)/shard_map/ppermute | solution.py:19
  52.9 7.8 %collective-permute-start.7 = (f32[40,4,384]{2,1,0:T(4,128)S(1)}, f32[40,4,384]{2,1,0:T(4,128)S(1)}, u32[]{:S(2)}, u32[]{:S(2)}) collective-permute-start(f32[40,4,384]{2,1,0:T(4,128)S(1)} %get-tuple-element.18), channel_id=1, source_target_pairs={{0,1},{1,2},{2,3},{4,5},{5,6},{6,7},{8,9},{9,10},{10,11},{12,13},{... | collective-permute-start | bytes 737288 | tf_op jit(solution)/shard_map/ppermute | solution.py:16
  91.5 17.7 %collective-permute-start.9 = (f32[4,64,384]{2,1,0:T(8,128)S(1)}, f32[4,64,384]{2,1,0:T(8,128)S(1)}, u32[]{:S(2)}, u32[]{:S(2)}) collective-permute-start(f32[4,64,384]{2,1,0:T(8,128)S(1)} %get-tuple-element.25), channel_id=1, source_target_pairs={{0,4},{4,8},{8,12},{12,16},{16,20},{20,24},{24,28},{1,5},{5,9},{9,... | collective-permute-start | bytes 1179656 | tf_op jit(solution)/shard_map/ppermute | solution.py:16
  95.6 13.5 %collective-permute-start.8 = (f32[4,64,384]{2,1,0:T(8,128)S(1)}, f32[4,64,384]{2,1,0:T(8,128)S(1)}, u32[]{:S(2)}, u32[]{:S(2)}) collective-permute-start(f32[4,64,384]{2,1,0:T(8,128)S(1)} %get-tuple-element.26), channel_id=1, source_target_pairs={{4,0},{8,4},{12,8},{16,12},{20,16},{24,20},{28,24},{5,1},{9,5},{13... | collective-permute-start | bytes 1179656 | tf_op jit(solution)/shard_map/ppermute | solution.py:19
  98.2 18.4 %collective-permute-start.2 = (f32[40,4,384]{2,1,0:T(4,128)S(1)}, f32[40,4,384]{2,1,0:T(4,128)S(1)}, u32[]{:S(2)}, u32[]{:S(2)}) collective-permute-start(f32[40,4,384]{2,1,0:T(4,128)S(1)} %get-tuple-element.21), channel_id=1, source_target_pairs={{1,0},{2,1},{3,2},{5,4},{6,5},{7,6},{9,8},{10,9},{11,10},{13,12},{... | collective-permute-start | bytes 737288 | tf_op jit(solution)/shard_map/ppermute | solution.py:19
  100.3 16.2 %collective-permute-start.3 = (f32[40,4,384]{2,1,0:T(4,128)S(1)}, f32[40,4,384]{2,1,0:T(4,128)S(1)}, u32[]{:S(2)}, u32[]{:S(2)}) collective-permute-start(f32[40,4,384]{2,1,0:T(4,128)S(1)} %get-tuple-element.22), channel_id=1, source_target_pairs={{0,1},{1,2},{2,3},{4,5},{5,6},{6,7},{8,9},{9,10},{10,11},{12,13},{... | collective-permute-start | bytes 737288 | tf_op jit(solution)/shard_map/ppermute | solution.py:16
  109.2 13.1 %collective-permute-start.10 = (f32[40,4,384]{2,1,0:T(4,128)S(1)}, f32[40,4,384]{2,1,0:T(4,128)S(1)}, u32[]{:S(2)}, u32[]{:S(2)}) collective-permute-start(f32[40,4,384]{2,1,0:T(4,128)S(1)} %get-tuple-element.13), channel_id=1, source_target_pairs={{1,0},{2,1},{3,2},{5,4},{6,5},{7,6},{9,8},{10,9},{11,10},{13,12},{... | collective-permute-start | bytes 737288 | tf_op jit(solution)/shard_map/ppermute | solution.py:19
  111.2 11.2 %collective-permute-start.11 = (f32[40,4,384]{2,1,0:T(4,128)S(1)}, f32[40,4,384]{2,1,0:T(4,128)S(1)}, u32[]{:S(2)}, u32[]{:S(2)}) collective-permute-start(f32[40,4,384]{2,1,0:T(4,128)S(1)} %get-tuple-element.14), channel_id=1, source_target_pairs={{0,1},{1,2},{2,3},{4,5},{5,6},{6,7},{8,9},{9,10},{10,11},{12,13},{... | collective-permute-start | bytes 737288 | tf_op jit(solution)/shard_map/ppermute | solution.py:16
  217.2 33.1 %copy-start.4 = (f32[32,64,384]{2,1,0:T(8,128)S(1)}, f32[32,64,384]{2,1,0:T(8,128)}, u32[]{:S(2)}) copy-start(f32[32,64,384]{2,1,0:T(8,128)} %fusion.106) | copy-start | bytes 9437188
  218.5 10.7 %collective-permute-start.12 = (f32[4,64,384]{2,1,0:T(8,128)S(1)}, f32[4,64,384]{2,1,0:T(8,128)S(1)}, u32[]{:S(2)}, u32[]{:S(2)}) collective-permute-start(f32[4,64,384]{2,1,0:T(8,128)S(1)} %get-tuple-element.23), channel_id=1, source_target_pairs={{4,0},{8,4},{12,8},{16,12},{20,16},{24,20},{28,24},{5,1},{9,5},{13... | collective-permute-start | bytes 1179656 | tf_op jit(solution)/shard_map/ppermute | solution.py:19
  219.8 18.6 %collective-permute-start.13 = (f32[4,64,384]{2,1,0:T(8,128)S(1)}, f32[4,64,384]{2,1,0:T(8,128)S(1)}, u32[]{:S(2)}, u32[]{:S(2)}) collective-permute-start(f32[4,64,384]{2,1,0:T(8,128)S(1)} %get-tuple-element.24), channel_id=1, source_target_pairs={{0,4},{4,8},{8,12},{12,16},{16,20},{20,24},{24,28},{1,5},{5,9},{9,... | collective-permute-start | bytes 1179656 | tf_op jit(solution)/shard_map/ppermute | solution.py:16
  239.8 9.0 %collective-permute-start.14 = (f32[40,4,384]{2,1,0:T(4,128)S(1)}, f32[40,4,384]{2,1,0:T(4,128)S(1)}, u32[]{:S(2)}, u32[]{:S(2)}) collective-permute-start(f32[40,4,384]{2,1,0:T(4,128)S(1)} %get-tuple-element.9), channel_id=1, source_target_pairs={{1,0},{2,1},{3,2},{5,4},{6,5},{7,6},{9,8},{10,9},{11,10},{13,12},{... | collective-permute-start | bytes 737288 | tf_op jit(solution)/shard_map/ppermute | solution.py:19
  241.9 8.3 %collective-permute-start.15 = (f32[40,4,384]{2,1,0:T(4,128)S(1)}, f32[40,4,384]{2,1,0:T(4,128)S(1)}, u32[]{:S(2)}, u32[]{:S(2)}) collective-permute-start(f32[40,4,384]{2,1,0:T(4,128)S(1)} %get-tuple-element.10), channel_id=1, source_target_pairs={{0,1},{1,2},{2,3},{4,5},{5,6},{6,7},{8,9},{9,10},{10,11},{12,13},{... | collective-permute-start | bytes 737288 | tf_op jit(solution)/shard_map/ppermute | solution.py:16
  286.6 80.6 %copy-start.8 = (f32[8,64,384]{2,1,0:T(8,128)S(1)}, f32[8,64,384]{2,1,0:T(8,128)}, u32[]{:S(2)}) copy-start(f32[8,64,384]{2,1,0:T(8,128)} %param.11) | copy-start | bytes 2359300
  286.6 80.6 %copy-start.9 = (f32[8,64,384]{2,1,0:T(8,128)S(1)}, f32[8,64,384]{2,1,0:T(8,128)}, u32[]{:S(2)}) copy-start(f32[8,64,384]{2,1,0:T(8,128)} %param.13) | copy-start | bytes 2359300
  286.6 80.6 %copy-start.10 = (f32[8,64,384]{2,1,0:T(8,128)S(1)}, f32[8,64,384]{2,1,0:T(8,128)}, u32[]{:S(2)}) copy-start(f32[8,64,384]{2,1,0:T(8,128)} %param.12) | copy-start | bytes 2359300
  (11 other events, 154.4 us)
Sparse Core Ops, SparseCore 0:
  9.7 42.9 all-gather.1
  286.8 80.3 all-reduce.5
where the time goes:
time: 377 us
  other arithmetic  174 us (46%)
  waiting for transfers between devices  124 us (33%)
  starting transfers between devices  55 us (15%)
  between operations  14.4 us (4%)
  local copies, waits for them, and re-layouts  8.33 us (2%)
    psum x1, waiting for transfers between devices, on_device(): full_sum = lax.psum(imaging, 'shot')  80.5 us
    reduce_sum x1, other arithmetic, on_device(): misfit_early = jnp.sum(advanced * receiver_mask, axis=2) - observed[0, 0]  45.6 us
    add x1, other arithmetic, on_device(): 2.0 * adj_now - adj_later + stiffness * laplace(padded_adjoint)  43.2 us
    ppermute x8, starting transfers between devices, extended(): lax.ppermute(lax.slice_in_dim(block, block.shape[dim] - width, None, axis...  41.2 us
    add x1, other arithmetic, on_device(): adj_two * (farthest - 2.0 * advanced + present)  32.6 us
    ppermute x8, waiting for transfers between devices, extended(): lax.ppermute(lax.slice_in_dim(block, block.shape[dim] - width, None, axis...  32.4 us
    add x1, other arithmetic, on_device(): 2.0 * present - oldest + stiffness * laplace(padded_wave)  23.5 us
    concatenate x4, other arithmetic, extended(): block = jnp.concatenate([low, block, high], axis=dim)  20 us
  transfers between devices with their start and end apart: 18, of which 10 were waited for; matrix products, arithmetic and copies ran while one was open for 12% of the time, Pallas kernels for 0%

commit v1 on v0

--- a/solution.py
+++ b/solution.py
@@ -1,3 +1,4 @@
+import functools
 import jax
 import jax.numpy as jnp
 from jax import lax
@@ -6,6 +7,14 @@
 STENCIL = (-205.0 / 72.0, 8.0 / 5.0, -1.0 / 5.0, 8.0 / 315.0, -1.0 / 560.0)
 squared_courant = 0.012
 leap_step = 0.2
+
+
+def _get_regions(frame, a_name):
+    w1 = jax.lax.all_gather(frame, axis_name=a_name)
+    return jnp.sum(w1, axis=0)
+
+
+play_sizes = functools.partial(_get_regions, a_name="shot")
 
 
 def extended(block, sides, width):
@@ -110,7 +119,7 @@
         advanced - 2.0 * present + oldest
     )
     share_rows = velocity.shape[0]
-    full_sum = lax.psum(imaging, "shot")
+    full_sum = play_sizes(imaging)
     summed = lax.dynamic_slice_in_dim(full_sum, lax.axis_index("shot") * share_rows, share_rows, 0)
     gradient = 2.0 / velocity * summed
     p_half = momentum - 0.5 * leap_step * gradient

time: 377 us -> 425 us (1.13)
  waiting for transfers between devices: 124 us -> 167 us
  other arithmetic: 174 us -> 180 us
    all_gather x0 -> x1, waiting for transfers between devices: none -> 123 us  [_get_regions(): w1 = jax.lax.all_gather(frame, axis_name=a_name)]
    psum x1 -> x0, waiting for transfers between devices: 80.5 us -> none  [on_device(): full_sum = lax.psum(imaging, 'shot')]
    reduce_sum x0 -> x1, other arithmetic: none -> 6.14 us  [_get_regions(): return jnp.sum(w1, axis=0)]
  transfers between devices with their start and end apart: 18 -> 18, of which waited for: 10 -> 10; matrix products, arithmetic and copies ran while one was open for 12% -> 11% of each run, Pallas kernels for 0% -> 0%
where the time goes in v1:
time: 425 us
  other arithmetic  180 us (42%)
  waiting for transfers between devices  167 us (39%)
  starting transfers between devices  55 us (13%)
  between operations  14.4 us (3%)
  local copies, waits for them, and re-layouts  8.35 us (2%)
    all_gather x1, waiting for transfers between devices, _get_regions(): w1 = jax.lax.all_gather(frame, axis_name=a_name)  123 us
    reduce_sum x1, other arithmetic, on_device(): misfit_early = jnp.sum(advanced * receiver_mask, axis=2) - observed[0, 0]  45.2 us
    add x1, other arithmetic, on_device(): 2.0 * adj_now - adj_later + stiffness * laplace(padded_adjoint)  43.3 us
    ppermute x8, starting transfers between devices, extended(): lax.ppermute(lax.slice_in_dim(block, block.shape[dim] - width, None, axis...  41.1 us
    add x1, other arithmetic, on_device(): adj_two * (farthest - 2.0 * advanced + present)  32.6 us
    ppermute x8, waiting for transfers between devices, extended(): lax.ppermute(lax.slice_in_dim(block, block.shape[dim] - width, None, axis...  32.4 us
    add x1, other arithmetic, on_device(): 2.0 * present - oldest + stiffness * laplace(padded_wave)  22.7 us
    concatenate x4, other arithmetic, extended(): block = jnp.concatenate([low, block, high], axis=dim)  19.9 us
  transfers between devices with their start and end apart: 18, of which 10 were waited for; matrix products, arithmetic and copies ran while one was open for 11% of the time, Pallas kernels for 0%

profile of v1, /device:TPU:1, one launch (start us, length us, event | category | flops | bytes accessed | tf_op | source)
XLA Modules:
  0.0 424.6 jit_solution(681743528998059546)
XLA Ops:
  11.5 5.4 %collective-permute-start.1 = (f32[4,64,384]{2,1,0:T(8,128)}, f32[4,64,384]{2,1,0:T(8,128)}, u32[]{:S(2)}, u32[]{:S(2)}) collective-permute-start(f32[4,64,384]{2,1,0:T(8,128)} %get-tuple-element.30), channel_id=1, source_target_pairs={{0,4},{4,8},{8,12},{12,16},{16,20},{20,24},{24,28},{1,5},{5,9},{9,... | collective-permute-start | bytes 1179656 | tf_op jit(solution)/shard_map/ppermute | solution.py:25
  20.3 4.9 %collective-permute-start.5 = (f32[4,64,384]{2,1,0:T(8,128)}, f32[4,64,384]{2,1,0:T(8,128)}, u32[]{:S(2)}, u32[]{:S(2)}) collective-permute-start(f32[4,64,384]{2,1,0:T(8,128)} %get-tuple-element.28), channel_id=1, source_target_pairs={{0,4},{4,8},{8,12},{12,16},{16,20},{20,24},{24,28},{1,5},{5,9},{9,... | collective-permute-start | bytes 1179656 | tf_op jit(solution)/shard_map/ppermute | solution.py:25
  27.9 3.1 collective-permute-done.4
  31.0 18.5 %collective-permute-done.5 = f32[4,64,384]{2,1,0:T(8,128)} collective-permute-done((f32[4,64,384]{2,1,0:T(8,128)}, f32[4,64,384]{2,1,0:T(8,128)}, u32[]{:S(2)}, u32[]{:S(2)}) %collective-permute-start.5) | collective-permute-done | bytes 393248 | tf_op jit(solution)/shard_map/ppermute | solution.py:25
  50.5 2.4 collective-permute-start.6
  52.9 4.7 %collective-permute-start.7 = (f32[40,4,384]{2,1,0:T(4,128)S(1)}, f32[40,4,384]{2,1,0:T(4,128)S(1)}, u32[]{:S(2)}, u32[]{:S(2)}) collective-permute-start(f32[40,4,384]{2,1,0:T(4,128)S(1)} %get-tuple-element.18), channel_id=1, source_target_pairs={{0,1},{1,2},{2,3},{4,5},{5,6},{6,7},{8,9},{9,10},{10,11},{12,13},{... | collective-permute-start | bytes 737288 | tf_op jit(solution)/shard_map/ppermute | solution.py:25
  60.7 5.9 %pad_maximum_fusion.1 = (f32[40,68,384]{2,1,0:T(8,128)}, f32[40,68,384]{2,1,0:T(8,128)}) fusion(f32[40,4,384]{2,1,0:T(4,128)S(1)} %collective-permute-done.6, f32[4,64,384]{2,1,0:T(8,128)} %collective-permute-done.4, f32[32,64,384]{2,1,0:T(8,128)S(1)} %bitcast.37, f32[4,64,384]{2,1,0:T(8,128)} %collective-permute-done.5, ...), kind=kLoop, calls=%fused_computation.59 | loop fusion | flops 6266880 | bytes 12779520 | tf_op jit(solution)/shard_map/concatenate | solution.py:29
  66.6 22.7 %fusion.75 = f32[32,64,384]{2,1,0:T(8,128)} fusion(f32[32,64,384]{2,1,0:T(8,128)S(1)} %bitcast.38, f32[4,64,384]{2,1,0:T(8,128)} %collective-permute-done.5, f32[4,64,384]{2,1,0:T(8,128)} %collective-permute-done.4, f32[40,68,384]{2,1,0:T(8,128)} %get-tuple-element.16, f32[40,68,384]{2,1,0:T(8,128)} %get-tuple-element.15, f32[1,32,64,384]{3,2,1,0:T(8,128)} %param.14, ...), kind=kLoop, calls=%fused_computation.166 | loop fusion | flops 36175872 | bytes 38537604 | tf_op jit(solution)/shard_map/add | solution.py:95
  90.6 4.1 collective-permute-start.9
  99.5 6.8 %collective-permute-start.3 = (f32[40,4,384]{2,1,0:T(4,128)S(1)}, f32[40,4,384]{2,1,0:T(4,128)S(1)}, u32[]{:S(2)}, u32[]{:S(2)}) collective-permute-start(f32[40,4,384]{2,1,0:T(4,128)S(1)} %get-tuple-element.22), channel_id=1, source_target_pairs={{0,1},{1,2},{2,3},{4,5},{5,6},{6,7},{8,9},{9,10},{10,11},{12,13},{... | collective-permute-start | bytes 737288 | tf_op jit(solution)/shard_map/ppermute | solution.py:25
  110.3 5.3 %collective-permute-start.11 = (f32[40,4,384]{2,1,0:T(4,128)S(1)}, f32[40,4,384]{2,1,0:T(4,128)S(1)}, u32[]{:S(2)}, u32[]{:S(2)}) collective-permute-start(f32[40,4,384]{2,1,0:T(4,128)S(1)} %get-tuple-element.14), channel_id=1, source_target_pairs={{0,1},{1,2},{2,3},{4,5},{5,6},{6,7},{8,9},{9,10},{10,11},{12,13},{... | collective-permute-start | bytes 737288 | tf_op jit(solution)/shard_map/ppermute | solution.py:25
  115.7 5.7 %pad_maximum_fusion = (f32[40,68,384]{2,1,0:T(8,128)}, f32[40,68,384]{2,1,0:T(8,128)}) fusion(f32[40,4,384]{2,1,0:T(4,128)S(1)} %collective-permute-done.2, f32[4,64,384]{2,1,0:T(8,128)S(1)} %collective-permute-done, f32[32,64,384]{2,1,0:T(8,128)S(1)} %bitcast.41, f32[4,64,384]{2,1,0:T(8,128)} %collective-permute-done.1, ...), kind=kLoop, calls=%fused_computation.57 | loop fusion | flops 6266880 | bytes 12779520 | tf_op jit(solution)/shard_map/concatenate | solution.py:29
  121.4 4.7 %pad_maximum_fusion.2 = (f32[40,68,384]{2,1,0:T(8,128)}, f32[40,68,384]{2,1,0:T(8,128)}) fusion(f32[40,4,384]{2,1,0:T(4,128)S(1)} %collective-permute-done.10, f32[4,64,384]{2,1,0:T(8,128)S(1)} %collective-permute-done.8, f32[32,64,384]{2,1,0:T(8,128)S(1)} %copy-done.1, f32[4,64,384]{2,1,0:T(8,128)S(1)} %collective-permute-done.9, ...), kind=kLoop, calls=%fused_computation.61 | loop fusion | flops 6266880 | bytes 12779520 | tf_op jit(solution)/shard_map/concatenate | solution.py:29
  126.1 45.2 %select_reduce_fusion = (f32[32,64]{1,0:T(8,128)}, f32[32,64]{1,0:T(8,128)}, f32[32,64,384]{2,1,0:T(8,128)}) fusion(f32[32,64,384]{2,1,0:T(8,128)} %fusion.75, s32[32,64]{1,0:T(8,128)S(1)} %bitcast.43, f32[]{:T(128)} %bitcast.13, pred[384]{0:T(512)(128)(4,1)} %copy-done.12, pred[32,64]{1,0:T(8,128)(4,1)} %copy-done.10, ...), kind=kLoop, calls=%fused_computation.252 | loop fusion | flops 40103936 | bytes 38562180 | tf_op jit(solution)/shard_map/reduce_sum | solution.py:105
  172.7 43.3 %fusion.106 = f32[32,64,384]{2,1,0:T(8,128)} fusion(f32[32,64,384]{2,1,0:T(8,128)} %bitcast.40, f32[4,64,384]{2,1,0:T(8,128)} %collective-permute-done.1, f32[4,64,384]{2,1,0:T(8,128)S(1)} %collective-permute-done, f32[40,68,384]{2,1,0:T(8,128)} %get-tuple-element.20, f32[40,68,384]{2,1,0:T(8,128)} %get-tuple-element.19, f32[1,32,64,384]{3,2,1,0:T(8,128)} %param.16, ...), kind=kLoop, calls=%fused_computation.197 | loop fusion | flops 36175872 | bytes 38551552 | tf_op jit(solution)/shard_map/add | solution.py:107
  218.6 4.5 %collective-permute-start.13 = (f32[4,64,384]{2,1,0:T(8,128)S(1)}, f32[4,64,384]{2,1,0:T(8,128)S(1)}, u32[]{:S(2)}, u32[]{:S(2)}) collective-permute-start(f32[4,64,384]{2,1,0:T(8,128)S(1)} %get-tuple-element.24), channel_id=1, source_target_pairs={{0,4},{4,8},{8,12},{12,16},{16,20},{20,24},{24,28},{1,5},{5,9},{9,... | collective-permute-start | bytes 1179656 | tf_op jit(solution)/shard_map/ppermute | solution.py:25
  223.1 4.9 %collective-permute-done.12 = f32[4,64,384]{2,1,0:T(8,128)S(1)} collective-permute-done((f32[4,64,384]{2,1,0:T(8,128)S(1)}, f32[4,64,384]{2,1,0:T(8,128)S(1)}, u32[]{:S(2)}, u32[]{:S(2)}) %collective-permute-start.12) | collective-permute-done | bytes 393248 | tf_op jit(solution)/shard_map/ppermute | solution.py:28
  228.0 9.2 %collective-permute-done.13 = f32[4,64,384]{2,1,0:T(8,128)S(1)} collective-permute-done((f32[4,64,384]{2,1,0:T(8,128)S(1)}, f32[4,64,384]{2,1,0:T(8,128)S(1)}, u32[]{:S(2)}, u32[]{:S(2)}) %collective-permute-start.13) | collective-permute-done | bytes 393248 | tf_op jit(solution)/shard_map/ppermute | solution.py:25
  240.7 5.4 %collective-permute-start.15 = (f32[40,4,384]{2,1,0:T(4,128)S(1)}, f32[40,4,384]{2,1,0:T(4,128)S(1)}, u32[]{:S(2)}, u32[]{:S(2)}) collective-permute-start(f32[40,4,384]{2,1,0:T(4,128)S(1)} %get-tuple-element.10), channel_id=1, source_target_pairs={{0,1},{1,2},{2,3},{4,5},{5,6},{6,7},{8,9},{9,10},{10,11},{12,13},{... | collective-permute-start | bytes 737288 | tf_op jit(solution)/shard_map/ppermute | solution.py:25
  249.1 3.7 pad_maximum_fusion.3
  252.7 32.6 %fusion.13 = f32[32,64,384]{2,1,0:T(8,128)} fusion(f32[32,64,384]{2,1,0:T(8,128)} %fusion.106, f32[4,64,384]{2,1,0:T(8,128)} %copy-done.7, f32[4,64,384]{2,1,0:T(8,128)S(1)} %collective-permute-done.12, f32[40,68,384]{2,1,0:T(8,128)} %get-tuple-element.8, f32[40,68,384]{2,1,0:T(8,128)S(1)} %get-tuple-element.7, f32[1,32,64,384]{3,2,1,0:T(8,128)} %param.14, ...), kind=kLoop, calls=%fused_computation.104 | loop fusion | flops 43253760 | bytes 51134464 | tf_op jit(solution)/shard_map/add | solution.py:118
  285.4 123.1 %all-gather.6.cloned.1.call-done = f32[128,64,384]{2,1,0:T(8,128)} async-done(((f32[32,64,384]{2,1,0:T(8,128)}), f32[128,64,384]{2,1,0:T(8,128)}) %all-gather.6.cloned.1.call-update) | async-done | bytes 12582928 | tf_op jit(solution)/shard_map/all_gather | solution.py:13
  408.5 6.1 %reduce_sum.29 = f32[32,64,384]{2,1,0:T(8,128)S(1)} reduce(f32[4,32,64,384]{3,2,1,0:T(8,128)} %bitcast.42, f32[]{:T(128)} %constant.14.clone.1), dimensions={0}, to_apply=%region_2.3 | reduce | flops 2359296 | bytes 15728644 | tf_op jit(solution)/shard_map/reduce_sum | solution.py:14
  414.7 3.0 divide_add_fusion
  (67 shorter events, 34.8 us)
Async XLA Ops:
  7.2 42.4 %copy-start = (f32[1,32,64,384]{3,2,1,0:T(8,128)S(1)}, f32[1,32,64,384]{3,2,1,0:T(8,128)}, u32[]{:S(2)}) copy-start(f32[1,32,64,384]{3,2,1,0:T(8,128)} %param.15) | copy-start | bytes 9437188
  7.2 20.0 %copy-start.13 = (f32[1,2]{1,0:T(1,128)S(1)}, f32[1,2]{1,0:T(1,128)}, u32[]{:S(2)}) copy-start(f32[1,2]{1,0:T(1,128)} %param.21) | copy-start | bytes 28
  7.2 59.4 %all-gather.4.cloned.1.call-start = ((), (), s32[]{:S(2)}) async-start(), calls=%async_computation | async-start | bytes 3932160 | tf_op jit(solution)/shard_map/all_gather | solution.py:76
  7.9 400.6 %all-gather.6.cloned.1.call-start = ((), (), s32[]{:S(2)}) async-start(), calls=%async_computation.1 | async-start | bytes 15728640 | tf_op jit(solution)/shard_map/all_gather | solution.py:13
  10.2 85.9 %collective-permute-start = (f32[4,64,384]{2,1,0:T(8,128)}, f32[4,64,384]{2,1,0:T(8,128)S(1)}, u32[]{:S(2)}, u32[]{:S(2)}) collective-permute-start(f32[4,64,384]{2,1,0:T(8,128)} %get-tuple-element.29), channel_id=1, source_target_pairs={{4,0},{8,4},{12,8},{16,12},{20,16},{24,20},{28,24},{5,1},{9,5},{13... | collective-permute-start | bytes 1179656 | tf_op jit(solution)/shard_map/ppermute | solution.py:28
  11.5 84.6 %collective-permute-start.1 = (f32[4,64,384]{2,1,0:T(8,128)}, f32[4,64,384]{2,1,0:T(8,128)}, u32[]{:S(2)}, u32[]{:S(2)}) collective-permute-start(f32[4,64,384]{2,1,0:T(8,128)} %get-tuple-element.30), channel_id=1, source_target_pairs={{0,4},{4,8},{8,12},{12,16},{16,20},{20,24},{24,28},{1,5},{5,9},{9,... | collective-permute-start | bytes 1179656 | tf_op jit(solution)/shard_map/ppermute | solution.py:25
  19.0 12.0 %collective-permute-start.4 = (f32[4,64,384]{2,1,0:T(8,128)}, f32[4,64,384]{2,1,0:T(8,128)}, u32[]{:S(2)}, u32[]{:S(2)}) collective-permute-start(f32[4,64,384]{2,1,0:T(8,128)} %get-tuple-element.27), channel_id=1, source_target_pairs={{4,0},{8,4},{12,8},{16,12},{20,16},{24,20},{28,24},{5,1},{9,5},{13... | collective-permute-start | bytes 1179656 | tf_op jit(solution)/shard_map/ppermute | solution.py:28
  20.3 29.2 %collective-permute-start.5 = (f32[4,64,384]{2,1,0:T(8,128)}, f32[4,64,384]{2,1,0:T(8,128)}, u32[]{:S(2)}, u32[]{:S(2)}) collective-permute-start(f32[4,64,384]{2,1,0:T(8,128)} %get-tuple-element.28), channel_id=1, source_target_pairs={{0,4},{4,8},{8,12},{12,16},{16,20},{20,24},{24,28},{1,5},{5,9},{9,... | collective-permute-start | bytes 1179656 | tf_op jit(solution)/shard_map/ppermute | solution.py:25
  26.5 40.1 %copy-start.12 = (pred[384]{0:T(512)(128)(4,1)}, pred[384]{0:T(512)(128)(4,1)S(1)}, u32[]{:S(2)}) copy-start(pred[384]{0:T(512)(128)(4,1)S(1)} %iota_compare_fusion.1) | copy-start | bytes 1156
  50.5 9.0 %collective-permute-start.6 = (f32[40,4,384]{2,1,0:T(4,128)S(1)}, f32[40,4,384]{2,1,0:T(4,128)S(1)}, u32[]{:S(2)}, u32[]{:S(2)}) collective-permute-start(f32[40,4,384]{2,1,0:T(4,128)S(1)} %get-tuple-element.17), channel_id=1, source_target_pairs={{1,0},{2,1},{3,2},{5,4},{6,5},{7,6},{9,8},{10,9},{11,10},{13,12},{... | collective-permute-start | bytes 737288 | tf_op jit(solution)/shard_map/ppermute | solution.py:28
  52.9 7.8 %collective-permute-start.7 = (f32[40,4,384]{2,1,0:T(4,128)S(1)}, f32[40,4,384]{2,1,0:T(4,128)S(1)}, u32[]{:S(2)}, u32[]{:S(2)}) collective-permute-start(f32[40,4,384]{2,1,0:T(4,128)S(1)} %get-tuple-element.18), channel_id=1, source_target_pairs={{0,1},{1,2},{2,3},{4,5},{5,6},{6,7},{8,9},{9,10},{10,11},{12,13},{... | collective-permute-start | bytes 737288 | tf_op jit(solution)/shard_map/ppermute | solution.py:25
  89.3 19.0 %copy-start.1 = (f32[32,64,384]{2,1,0:T(8,128)S(1)}, f32[32,64,384]{2,1,0:T(8,128)}, u32[]{:S(2)}) copy-start(f32[32,64,384]{2,1,0:T(8,128)} %fusion.75) | copy-start | bytes 9437188
  90.6 17.7 %collective-permute-start.9 = (f32[4,64,384]{2,1,0:T(8,128)S(1)}, f32[4,64,384]{2,1,0:T(8,128)S(1)}, u32[]{:S(2)}, u32[]{:S(2)}) collective-permute-start(f32[4,64,384]{2,1,0:T(8,128)S(1)} %get-tuple-element.25), channel_id=1, source_target_pairs={{0,4},{4,8},{8,12},{12,16},{16,20},{20,24},{24,28},{1,5},{5,9},{9,... | collective-permute-start | bytes 1179656 | tf_op jit(solution)/shard_map/ppermute | solution.py:25
  94.8 13.5 %collective-permute-start.8 = (f32[4,64,384]{2,1,0:T(8,128)S(1)}, f32[4,64,384]{2,1,0:T(8,128)S(1)}, u32[]{:S(2)}, u32[]{:S(2)}) collective-permute-start(f32[4,64,384]{2,1,0:T(8,128)S(1)} %get-tuple-element.26), channel_id=1, source_target_pairs={{4,0},{8,4},{12,8},{16,12},{20,16},{24,20},{28,24},{5,1},{9,5},{13... | collective-permute-start | bytes 1179656 | tf_op jit(solution)/shard_map/ppermute | solution.py:28
  97.3 18.4 %copy-start.3 = (f32[1,32,64,384]{3,2,1,0:T(8,128)S(1)}, f32[1,32,64,384]{3,2,1,0:T(8,128)}, u32[]{:S(2)}) copy-start(f32[1,32,64,384]{3,2,1,0:T(8,128)} %param.17) | copy-start | bytes 9437188
  97.3 18.4 %collective-permute-start.2 = (f32[40,4,384]{2,1,0:T(4,128)S(1)}, f32[40,4,384]{2,1,0:T(4,128)S(1)}, u32[]{:S(2)}, u32[]{:S(2)}) collective-permute-start(f32[40,4,384]{2,1,0:T(4,128)S(1)} %get-tuple-element.21), channel_id=1, source_target_pairs={{1,0},{2,1},{3,2},{5,4},{6,5},{7,6},{9,8},{10,9},{11,10},{13,12},{... | collective-permute-start | bytes 737288 | tf_op jit(solution)/shard_map/ppermute | solution.py:28
  99.5 16.2 %collective-permute-start.3 = (f32[40,4,384]{2,1,0:T(4,128)S(1)}, f32[40,4,384]{2,1,0:T(4,128)S(1)}, u32[]{:S(2)}, u32[]{:S(2)}) collective-permute-start(f32[40,4,384]{2,1,0:T(4,128)S(1)} %get-tuple-element.22), channel_id=1, source_target_pairs={{0,1},{1,2},{2,3},{4,5},{5,6},{6,7},{8,9},{9,10},{10,11},{12,13},{... | collective-permute-start | bytes 737288 | tf_op jit(solution)/shard_map/ppermute | solution.py:25
  108.4 13.0 %collective-permute-start.10 = (f32[40,4,384]{2,1,0:T(4,128)S(1)}, f32[40,4,384]{2,1,0:T(4,128)S(1)}, u32[]{:S(2)}, u32[]{:S(2)}) collective-permute-start(f32[40,4,384]{2,1,0:T(4,128)S(1)} %get-tuple-element.13), channel_id=1, source_target_pairs={{1,0},{2,1},{3,2},{5,4},{6,5},{7,6},{9,8},{10,9},{11,10},{13,12},{... | collective-permute-start | bytes 737288 | tf_op jit(solution)/shard_map/ppermute | solution.py:28
  110.3 11.1 %collective-permute-start.11 = (f32[40,4,384]{2,1,0:T(4,128)S(1)}, f32[40,4,384]{2,1,0:T(4,128)S(1)}, u32[]{:S(2)}, u32[]{:S(2)}) collective-permute-start(f32[40,4,384]{2,1,0:T(4,128)S(1)} %get-tuple-element.14), channel_id=1, source_target_pairs={{0,1},{1,2},{2,3},{4,5},{5,6},{6,7},{8,9},{9,10},{10,11},{12,13},{... | collective-permute-start | bytes 737288 | tf_op jit(solution)/shard_map/ppermute | solution.py:25
  216.0 33.1 %copy-start.4 = (f32[32,64,384]{2,1,0:T(8,128)S(1)}, f32[32,64,384]{2,1,0:T(8,128)}, u32[]{:S(2)}) copy-start(f32[32,64,384]{2,1,0:T(8,128)} %fusion.106) | copy-start | bytes 9437188
  217.3 10.7 %collective-permute-start.12 = (f32[4,64,384]{2,1,0:T(8,128)S(1)}, f32[4,64,384]{2,1,0:T(8,128)S(1)}, u32[]{:S(2)}, u32[]{:S(2)}) collective-permute-start(f32[4,64,384]{2,1,0:T(8,128)S(1)} %get-tuple-element.23), channel_id=1, source_target_pairs={{4,0},{8,4},{12,8},{16,12},{20,16},{24,20},{28,24},{5,1},{9,5},{13... | collective-permute-start | bytes 1179656 | tf_op jit(solution)/shard_map/ppermute | solution.py:28
  218.6 18.6 %collective-permute-start.13 = (f32[4,64,384]{2,1,0:T(8,128)S(1)}, f32[4,64,384]{2,1,0:T(8,128)S(1)}, u32[]{:S(2)}, u32[]{:S(2)}) collective-permute-start(f32[4,64,384]{2,1,0:T(8,128)S(1)} %get-tuple-element.24), channel_id=1, source_target_pairs={{0,4},{4,8},{8,12},{12,16},{16,20},{20,24},{24,28},{1,5},{5,9},{9,... | collective-permute-start | bytes 1179656 | tf_op jit(solution)/shard_map/ppermute | solution.py:25
  238.6 9.0 %collective-permute-start.14 = (f32[40,4,384]{2,1,0:T(4,128)S(1)}, f32[40,4,384]{2,1,0:T(4,128)S(1)}, u32[]{:S(2)}, u32[]{:S(2)}) collective-permute-start(f32[40,4,384]{2,1,0:T(4,128)S(1)} %get-tuple-element.9), channel_id=1, source_target_pairs={{1,0},{2,1},{3,2},{5,4},{6,5},{7,6},{9,8},{10,9},{11,10},{13,12},{... | collective-permute-start | bytes 737288 | tf_op jit(solution)/shard_map/ppermute | solution.py:28
  240.7 8.3 %collective-permute-start.15 = (f32[40,4,384]{2,1,0:T(4,128)S(1)}, f32[40,4,384]{2,1,0:T(4,128)S(1)}, u32[]{:S(2)}, u32[]{:S(2)}) collective-permute-start(f32[40,4,384]{2,1,0:T(4,128)S(1)} %get-tuple-element.10), channel_id=1, source_target_pairs={{0,1},{1,2},{2,3},{4,5},{5,6},{6,7},{8,9},{9,10},{10,11},{12,13},{... | collective-permute-start | bytes 737288 | tf_op jit(solution)/shard_map/ppermute | solution.py:25
  (8 other events, 96.8 us)
Sparse Core Ops, SparseCore 0:
  9.7 42.9 all-gather.3
  285.5 122.9 all-gather.5
